TPU v7x, 32 devices: a whole 2x2x4 slice. The times are simulated.
32 devices in a mesh: groups: 2 (over y), frame: 8 (over z, x), row: 2 (over core).
Axes of the slice: x: 2, y: 2, z: 4, core: 2. Of those that a mesh axis runs over, the one named last changes fastest.
Arguments:
- latent: bfloat16 [16, 16, 64, 640], P(('groups', 'frame'), 'row'), parts along dimension 0, may hold values from -18 to 18
- norm_gain: float32 [640], replicated, may hold values from 0.1 to 1.9
- time_kernel: bfloat16 [3, 640, 640], replicated, may hold values from -0.125 to 0.125
- space_norm: float32 [640], replicated, may hold values from 0.1 to 1.9
- space_qkv: bfloat16 [640, 1920], replicated, may hold values from -12 to 12
- space_out: bfloat16 [640, 640], replicated, may hold values from -0.25 to 0.25
- time_norm: float32 [640], replicated, may hold values from 0.1 to 1.9
- time_qkv: bfloat16 [640, 1920], replicated, may hold values from -12 to 12
- time_out: bfloat16 [640, 640], replicated, may hold values from -0.25 to 0.25
Outputs:
- output: float32 [16, 16, 64, 640], P(('groups', 'frame'), 'row'), parts along dimension 0
There are 2 independent parts, one for each index of `groups`. A program takes and returns all parts, laid end to end along the dimension named above; an argument that names none is the same for every part. Nothing has to cross between parts.
All inputs are finite; a program needn't handle non-finite values.
Results may differ from a plain program's by a relative error of at most 0.0018.
Values may be sent and summed in bfloat16 or wider, within the bound.
A program may use at most 128 MiB of HBM per device.

v0:
```python
import jax
import jax.numpy as jnp
from jax import lax
from jax.sharding import PartitionSpec as P

HEADS = 10
GROUPS = 32


epsilon = 1e-05


def padded_2(block, sides, width):
    for axis, dim in sides:
        count = lax.axis_size(axis)
        forward = [(i, i + 1) for i in range(count - 1)]
        backward = [(target, source) for source, target in forward]
        low = lax.ppermute(
            lax.slice_in_dim(block, block.shape[dim] - width, None, axis=dim), axis, forward
        )
        high = lax.ppermute(lax.slice_in_dim(block, 0, width, axis=dim), axis, backward)
        block = jnp.concatenate([low, block, high], axis=dim)
    return block


def normalize_silu(grouped, first, second, number, gain, shape):
    center = first / number
    spread = second / number - center * center
    scaling = lax.rsqrt(spread + epsilon)
    normed = ((grouped - center[:, None]) * scaling[:, None]).reshape(shape) * gain
    return jax.nn.silu(normed).astype(jnp.bfloat16)


def layer_norm(inputs, gain):
    center = jnp.mean(inputs, axis=-1, keepdims=True)
    shifted = inputs - center
    spread = jnp.mean(shifted * shifted, axis=-1, keepdims=True)
    return (shifted * lax.rsqrt(spread + epsilon) * gain).astype(jnp.bfloat16)


def project_three(inputs, weight):
    channels = weight.shape[0]
    lead = inputs.shape[:-1]
    packed = jnp.dot(
        inputs.reshape(-1, channels), weight, preferred_element_type=jnp.float32
    ).astype(jnp.bfloat16)
    packed = packed.reshape(lead + (3 * channels,))
    return (
        packed[..., :channels],
        packed[..., channels : 2 * channels],
        packed[..., 2 * channels :],
    )


def time_attend(queries, key_rows, values):
    frames, pixels, channels = queries.shape
    head_size = channels // HEADS
    query_heads = queries.reshape(frames, pixels, HEADS, head_size)
    key_heads = key_rows.reshape(frames, pixels, HEADS, head_size)
    value_heads = values.reshape(frames, pixels, HEADS, head_size)
    scores = jnp.einsum(
        "qphd,kphd->phqk", query_heads, key_heads, preferred_element_type=jnp.float32
    ) * head_size ** (-0.5)
    raised = jnp.exp(scores - jnp.max(scores, axis=-1, keepdims=True))
    weight_sum = jnp.sum(raised, axis=-1)
    weights = raised.astype(jnp.bfloat16)
    result = jnp.einsum("phqk,kphd->qphd", weights, value_heads, preferred_element_type=jnp.float32)
    result = result / jnp.transpose(weight_sum, (2, 0, 1))[:, :, :, None]
    return result.astype(jnp.bfloat16).reshape(frames, pixels, channels)


def add_projected(base, attended, weight):
    channels = weight.shape[0]
    summed = base.reshape(-1, channels) + jnp.dot(
        attended.reshape(-1, channels), weight, preferred_element_type=jnp.float32
    )
    return summed.reshape(base.shape)


def body(
    latent, norm_gain, time_kernel, space_norm, space_qkv, space_out, time_norm, time_qkv, time_out
):
    frames, row_count, col_count, channels = latent.shape
    pixels = row_count * col_count
    per_group = channels // GROUPS
    head_size = channels // HEADS
    grouped = latent.astype(jnp.float32).reshape(frames, row_count, col_count, GROUPS, per_group)
    first = jnp.sum(grouped, axis=(0, 1, 2, 4))
    second = jnp.sum(grouped * grouped, axis=(0, 1, 2, 4))
    first, second = lax.psum((first, second), ("frame", "row"))
    number = frames * lax.axis_size("frame") * pixels * lax.axis_size("row") * per_group
    hidden = normalize_silu(grouped, first, second, number, norm_gain, latent.shape)
    padded = padded_2(hidden, (("frame", 0),), 1)
    mixed = jnp.zeros((frames * pixels, channels), jnp.float32)
    for tap in range(3):
        window = padded[tap : tap + frames].reshape(-1, channels)
        mixed = mixed + jnp.dot(window, time_kernel[tap], preferred_element_type=jnp.float32)
    stepped = latent.astype(jnp.float32).reshape(-1, channels) + mixed
    stepped = stepped.reshape(frames, pixels, channels)
    tokens = layer_norm(stepped, space_norm)
    queries, key_rows, values = project_three(tokens, space_qkv)
    query_heads = queries.reshape(frames, pixels, HEADS, head_size)
    top_score = jnp.full((frames, HEADS, pixels), -jnp.inf, jnp.float32)
    weight_sum = jnp.zeros((frames, HEADS, pixels), jnp.float32)
    partial_sum = jnp.zeros((frames, HEADS, pixels, head_size), jnp.float32)
    key_piece = lax.all_gather(key_rows, "row", axis=1, tiled=True)
    value_piece = lax.all_gather(values, "row", axis=1, tiled=True)
    key_count = key_piece.shape[1]
    key_heads = key_piece.reshape(frames, key_count, HEADS, head_size)
    value_heads = value_piece.reshape(frames, key_count, HEADS, head_size)
    scores = jnp.einsum(
        "fqhd,fkhd->fhqk", query_heads, key_heads, preferred_element_type=jnp.float32
    ) * head_size ** (-0.5)
    new_top = jnp.max(scores, axis=-1)
    rescale = jnp.exp(top_score - new_top)
    raised = jnp.exp(scores - new_top[..., None])
    weight_sum = weight_sum * rescale + jnp.sum(raised, axis=-1)
    weights = raised.astype(jnp.bfloat16)
    partial_sum = partial_sum * rescale[..., None] + jnp.einsum(
        "fhqk,fkhd->fhqd", weights, value_heads, preferred_element_type=jnp.float32
    )
    top_score, weight_sum, partial_sum = (new_top, weight_sum, partial_sum)
    attended = (partial_sum / weight_sum[..., None]).astype(jnp.bfloat16)
    attended = jnp.transpose(attended, (0, 2, 1, 3)).reshape(frames, pixels, channels)
    spaced = add_projected(stepped, attended, space_out)
    moved = lax.all_to_all(spaced, "frame", split_axis=1, concat_axis=0, tiled=True)
    normed = layer_norm(moved, time_norm)
    queries, key_rows, values = project_three(normed, time_qkv)
    result = time_attend(queries, key_rows, values)
    finished = add_projected(moved, result, time_out)
    output = lax.all_to_all(finished, "frame", split_axis=0, concat_axis=1, tiled=True)
    return output.reshape(frames, row_count, col_count, channels)


def solution(mesh):
    return jax.shard_map(
        body,
        mesh=mesh,
        in_specs=(
            P(("groups", "frame"), "row", None, None),
            P(),
            P(),
            P(),
            P(),
            P(),
            P(),
            P(),
            P(),
        ),
        out_specs=P(("groups", "frame"), "row", None, None),
        check_vma=False,
    )
```

profile of v0, /device:TPU:0, one launch (start us, length us, event | category | flops | bytes accessed | tf_op | source)
XLA Modules:
  0.0 232.8 jit_solution(14657514073746604664)
XLA Ops:
  8.4 34.9 %all-reduce = (f32[32]{0:T(128)S(1)}, f32[32]{0:T(128)S(1)}) all-reduce(f32[32]{0:T(128)S(1)} %reduce_sum.91, f32[32]{0:T(128)S(1)} %reduce_sum.88), channel_id=1, replica_groups=mesh['groups'=2,'frame'=8,'row'=2] {'frame','row'}, use_global_device_ids=true, to_apply=%region_5.6 | all-reduce | flops 64 | bytes 512 | tf_op jit(solution)/shard_map/psum | solution.py:90
  46.5 4.6 %collective-permute-start = (bf16[1,8,64,640]{3,2,1,0:T(8,128)(2,1)S(1)}, bf16[1,8,64,640]{3,2,1,0:T(8,128)(2,1)S(1)}, u32[]{:S(2)}, u32[]{:S(2)}) collective-permute-start(bf16[1,8,64,640]{3,2,1,0:T(8,128)(2,1)S(1)} %multiply_convert_fusion.1), channel_id=1, source_target_pairs={{0,2},{2,4},{4,6},{6,8},{8,10},{10,12},{12,14},{1,3},{3,5},{5,7},{... | collective-permute-start | bytes 1966088 | tf_op jit(solution)/shard_map/ppermute | solution.py:18
  51.1 2.0 fusion.24
  53.2 6.7 %collective-permute-done.1 = bf16[1,8,64,640]{3,2,1,0:T(8,128)(2,1)S(1)} collective-permute-done((bf16[1,8,64,640]{3,2,1,0:T(8,128)(2,1)S(1)}, bf16[1,8,64,640]{3,2,1,0:T(8,128)(2,1)S(1)}, u32[]{:S(2)}, u32[]{:S(2)}) %collective-permute-start.1) | collective-permute-done | bytes 655392 | tf_op jit(solution)/shard_map/ppermute | solution.py:21
  60.6 8.8 %collective-permute-done = bf16[1,8,64,640]{3,2,1,0:T(8,128)(2,1)S(1)} collective-permute-done((bf16[1,8,64,640]{3,2,1,0:T(8,128)(2,1)S(1)}, bf16[1,8,64,640]{3,2,1,0:T(8,128)(2,1)S(1)}, u32[]{:S(2)}, u32[]{:S(2)}) %collective-permute-start) | collective-permute-done | bytes 655392 | tf_op jit(solution)/shard_map/ppermute | solution.py:18
  71.0 1.9 fusion.4
  74.9 10.5 %all-gather.3.cloned.1.call-done = bf16[1,1024,640]{2,1,0:T(8,128)(2,1)} async-done(((bf16[1,512,640]{2,1,0:T(8,128)(2,1)}), bf16[1,1024,640]{2,1,0:T(8,128)(2,1)}) %all-gather.3.cloned.1.call-update) | async-done | bytes 1310736 | tf_op jit(solution)/shard_map/all_gather | solution.py:106
  87.0 3.0 %multiply_reduce_fusion = (f32[10,512]{1,0:T(8,128)S(1)}, f32[10,512,1024]{2,1,0:T(8,128)S(1)}) fusion(bf16[512,10,64]{0,2,1:T(8,128)(2,1)S(1)} %bitcast.75, bf16[1024,10,64]{0,2,1:T(8,128)(2,1)S(1)} %bitcast.69), kind=kOutput, calls=%fused_computation.1 | convolution fusion | flops 681569280 | bytes 22958080 | tf_op jit(solution)/shard_map/fqhd,fkhd->fhqk/dot_general | solution.py:111
  90.0 4.6 %fusion = f32[10,512]{1,0:T(8,128)S(1)} fusion(f32[10,512,1024]{2,1,0:T(8,128)S(1)} %get-tuple-element.22, f32[10,512]{1,0:T(8,128)S(1)} %get-tuple-element.21), kind=kLoop, calls=%fused_computation.2 | loop fusion | flops 15723520 | bytes 21012480 | tf_op jit(solution)/shard_map/reduce_sum | solution.py:117
  94.6 3.0 %copy-done.2 = f32[10,512,1024]{2,1,0:T(8,128)} copy-done((f32[10,512,1024]{2,1,0:T(8,128)}, f32[10,512,1024]{2,1,0:T(8,128)S(1)}, u32[]{:S(2)}) %copy-start.2) | copy-done | bytes 20971544
  97.6 2.5 %copy.27 = bf16[1,1024,640]{1,2,0:T(8,128)(2,1)} copy(bf16[1,1024,640]{2,1,0:T(8,128)(2,1)} %all-gather.5.cloned.1.call-done) | data formatting | bytes 2621440 | tf_op jit(solution)/shard_map/all_gather | solution.py:107
  100.2 9.5 %divide_convert_fusion = bf16[10,512,64]{1,2,0:T(8,128)(2,1)S(1)} fusion(bf16[1024,10,64]{0,2,1:T(8,128)(2,1)} %bitcast.78, f32[10,512,1024]{2,1,0:T(8,128)} %copy-done.2, f32[10,512]{1,0:T(8,128)S(1)} %get-tuple-element.21, f32[10,512]{1,0:T(8,128)S(1)} %get-tuple-element.16, f32[10,512]{1,0:T(8,128)S(1)} %get-tuple-element.15), kind=kOutput, calls=%fused_computation.28 | convolution fusion | flops 687800320 | bytes 22999040 | tf_op jit(solution)/shard_map/fhqk,fkhd->fhqd/dot_general | solution.py:119
  111.9 37.4 %all_to_all.8 = f32[1,512,640]{2,0,1:T(1,128)S(1)} all-to-all(f32[1,512,640]{2,0,1:T(1,128)S(1)} %copy.28), channel_id=1, replica_groups=mesh['groups'=2,'frame'=8,'row'=2] {'frame'}, dimensions={1} | all-to-all | bytes 2621440 | tf_op jit(solution)/shard_map/all_to_all | solution.py:126
  150.9 7.6 %multiply_reduce_fusion.2 = f32[512]{0:T(512)S(1)} fusion(f32[1,512,640]{2,0,1:T(1,128)S(1)} %all_to_all.8, f32[512]{0:T(512)S(1)} %broadcast_multiply_fusion), kind=kLoop, calls=%fused_computation.27 | loop fusion | flops 982528 | bytes 1314816 | tf_op jit(solution)/shard_map/reduce_sum | solution.py:37
  158.5 3.6 %convolution_convert_fusion = bf16[512,1920]{1,0:T(8,128)(2,1)S(1)} fusion(bf16[640,1920]{1,0:T(8,128)(2,1)} %param.16, f32[1,512,640]{2,0,1:T(1,128)S(1)} %all_to_all.8, f32[640]{0:T(1024)S(1)} %copy-done.11, f32[512]{0:T(512)S(1)} %add_rsqrt_fusion, f32[512]{0:T(512)S(1)} %broadcast_multiply_fusion), kind=kOutput, calls=%fused_computation.5 | convolution fusion | flops 1260584960 | bytes 5741056 | tf_op jit(solution)/shard_map/dot_general | solution.py:44
  163.2 2.3 copy.40
  165.5 2.6 %copy.32 = bf16[8,64,10,64]{3,0,2,1:T(8,128)(2,1)} copy(bf16[8,64,10,64]{1,3,2,0:T(8,128)(2,1)} %bitcast.71) | data formatting | bytes 1310720 | tf_op jit(solution)/shard_map/reshape | solution.py:58
  169.6 2.6 %copy.33 = bf16[8,64,10,64]{3,0,2,1:T(8,128)(2,1)} copy(bf16[8,64,10,64]{1,3,2,0:T(8,128)(2,1)} %bitcast.72) | data formatting | bytes 1310720 | tf_op jit(solution)/shard_map/reshape | solution.py:59
  173.6 2.7 %copy.34 = bf16[8,64,10,64]{3,0,2,1:T(8,128)(2,1)} copy(bf16[8,64,10,64]{1,3,2,0:T(8,128)(2,1)} %bitcast.73) | data formatting | bytes 1310720 | tf_op jit(solution)/shard_map/reshape | solution.py:60
  176.3 2.9 %multiply_reduce_fusion.1 = (f32[64,10,8]{2,1,0:T(8,128)S(1)}, f32[64,10,8,8]{2,3,1,0:T(8,128)S(1)}) fusion(bf16[8,64,10,64]{3,0,2,1:T(8,128)(2,1)} %copy.32, bf16[8,64,10,64]{3,0,2,1:T(8,128)(2,1)} %copy.33), kind=kOutput, calls=%fused_computation.11 | convolution fusion | flops 5319680 | bytes 1495040 | tf_op jit(solution)/shard_map/qphd,kphd->phqk/dot_general | solution.py:61
  180.4 2.5 %fusion.5 = bf16[8,64,10,64]{3,0,2,1:T(8,128)(2,1)} fusion(bf16[8,64,10,64]{3,0,2,1:T(8,128)(2,1)S(1)} %copy-done.7, f32[64,10,8,8]{2,3,1,0:T(8,128)S(1)} %get-tuple-element.24, f32[8,64,10]{0,2,1:T(8,128)S(1)} %bitcast.82, f32[64,10,8]{2,1,0:T(8,128)S(1)} %get-tuple-element.23), kind=kOutput, calls=%fused_computation.9 | convolution fusion | flops 6021120 | bytes 1515520 | tf_op jit(solution)/shard_map/phqk,kphd->qphd/dot_general | solution.py:67
  182.9 3.0 %copy.36 = bf16[8,64,10,64]{1,0,3,2:T(8,128)(2,1)} copy(bf16[8,64,10,64]{3,0,2,1:T(8,128)(2,1)} %fusion.5) | data formatting | bytes 1310720 | tf_op jit(solution)/shard_map/convert_element_type | solution.py:69
  186.0 2.1 reshape_reshape.7
  188.9 34.8 %all_to_all.9 = f32[8,64,640]{2,1,0:T(8,128)S(1)} all-to-all(f32[8,64,640]{2,1,0:T(8,128)S(1)} %bitcast.70), channel_id=1, replica_groups=mesh['groups'=2,'frame'=8,'row'=2] {'frame'}, dimensions={0} | all-to-all | bytes 2621440 | tf_op jit(solution)/shard_map/all_to_all | solution.py:131
  (60 shorter events, 23.0 us)
Async XLA Ops:
  6.5 64.1 %copy-start = (bf16[640,1920]{1,0:T(8,128)(2,1)S(1)}, bf16[640,1920]{1,0:T(8,128)(2,1)}, u32[]{:S(2)}) copy-start(bf16[640,1920]{1,0:T(8,128)(2,1)} %param.13) | copy-start | bytes 7372804
  6.5 78.8 %all-gather.3.cloned.1.call-start = ((), (), s32[]{:S(2)}) async-start(), calls=%async_computation.2 | async-start | bytes 1966080 | tf_op jit(solution)/shard_map/all_gather | solution.py:106
  45.2 14.6 %collective-permute-start.1 = (bf16[1,8,64,640]{3,2,1,0:T(8,128)(2,1)S(1)}, bf16[1,8,64,640]{3,2,1,0:T(8,128)(2,1)S(1)}, u32[]{:S(2)}, u32[]{:S(2)}) collective-permute-start(bf16[1,8,64,640]{3,2,1,0:T(8,128)(2,1)S(1)} %multiply_convert_fusion.1), channel_id=1, source_target_pairs={{2,0},{4,2},{6,4},{8,6},{10,8},{12,10},{14,12},{3,1},{5,3},{7,5},{... | collective-permute-start | bytes 1966088 | tf_op jit(solution)/shard_map/ppermute | solution.py:21
  46.5 22.9 %collective-permute-start = (bf16[1,8,64,640]{3,2,1,0:T(8,128)(2,1)S(1)}, bf16[1,8,64,640]{3,2,1,0:T(8,128)(2,1)S(1)}, u32[]{:S(2)}, u32[]{:S(2)}) collective-permute-start(bf16[1,8,64,640]{3,2,1,0:T(8,128)(2,1)S(1)} %multiply_convert_fusion.1), channel_id=1, source_target_pairs={{0,2},{2,4},{4,6},{6,8},{8,10},{10,12},{12,14},{1,3},{3,5},{5,7},{... | collective-permute-start | bytes 1966088 | tf_op jit(solution)/shard_map/ppermute | solution.py:18
  51.1 8.8 %copy-start.6 = (bf16[3,640,640]{2,1,0:T(8,128)(2,1)S(1)}, bf16[3,640,640]{2,1,0:T(8,128)(2,1)}, u32[]{:S(2)}) copy-start(bf16[3,640,640]{2,1,0:T(8,128)(2,1)} %param.11) | copy-start | bytes 7372804
  59.9 9.5 %copy-start.5 = (bf16[1,8,64,640]{3,2,1,0:T(8,128)(2,1)S(1)}, bf16[1,8,64,640]{3,2,1,0:T(8,128)(2,1)}, u32[]{:S(2)}) copy-start(bf16[1,8,64,640]{3,2,1,0:T(8,128)(2,1)} %param.9) | copy-start | bytes 1966084
  70.3 2.6 %copy-start.3 = (f32[512,640]{1,0:T(8,128)}, f32[512,640]{1,0:T(8,128)S(1)}, u32[]{:S(2)}) copy-start(f32[512,640]{1,0:T(8,128)S(1)} %get-tuple-element.20) | copy-start | bytes 3932164
  70.3 0.7 copy-start.10
  74.2 23.5 %all-gather.5.cloned.1.call-start = ((), (), s32[]{:S(2)}) async-start(), calls=%async_computation.3 | async-start | bytes 1966080 | tf_op jit(solution)/shard_map/all_gather | solution.py:107
  90.0 7.6 %copy-start.2 = (f32[10,512,1024]{2,1,0:T(8,128)}, f32[10,512,1024]{2,1,0:T(8,128)S(1)}, u32[]{:S(2)}) copy-start(f32[10,512,1024]{2,1,0:T(8,128)S(1)} %get-tuple-element.22) | copy-start | bytes 62914564
  100.2 9.5 %copy-start.4 = (f32[512,640]{1,0:T(8,128)S(1)}, f32[512,640]{1,0:T(8,128)}, u32[]{:S(2)}) copy-start(f32[512,640]{1,0:T(8,128)} %copy-done.3) | copy-start | bytes 3932164
  100.2 9.6 %copy-start.8 = (bf16[640,640]{1,0:T(8,128)(2,1)S(1)}, bf16[640,640]{1,0:T(8,128)(2,1)}, u32[]{:S(2)}) copy-start(bf16[640,640]{1,0:T(8,128)(2,1)} %param.14) | copy-start | bytes 2457604
  149.3 9.3 %copy-start.11 = (f32[640]{0:T(1024)S(1)}, f32[640]{0:T(1024)}, u32[]{:S(2)}) copy-start(f32[640]{0:T(1024)} %param.15) | copy-start | bytes 7684
  179.1 1.3 copy-start.7
  186.0 2.1 copy-start.9
  223.8 2.2 copy-start.1
Sparse Core Ops, SparseCore 0:
  74.3 11.0 all-gather.2
  86.9 10.5 all-gather.4
where the time goes:
time: 233 us
  blocking collectives  107 us (46%)
  local copies, waits for them, and re-layouts  32.5 us (14%)
  matrix products  28.6 us (12%)
  waiting for transfers between devices  26.2 us (11%)
  other arithmetic  18.6 us (8%)
  between operations  13.7 us (6%)
  starting transfers between devices  6.1 us (3%)
    all_to_all x1, blocking collectives, body(): lax.all_to_all(spaced, 'frame', split_axis=1, concat_axis=0, tiled=True)  37.4 us
    psum x1, blocking collectives, body(): first, second = lax.psum((first, second), ('frame', 'row'))  34.9 us
    all_to_all x1, blocking collectives, body(): lax.all_to_all(finished, 'frame', split_axis=0, concat_axis=1, tiled=True)  34.8 us
    unnamed x28, local copies, waits for them, and re-layouts  10.8 us
    all_gather x1, waiting for transfers between devices, body(): key_piece = lax.all_gather(key_rows, 'row', axis=1, tiled=True)  10.5 us
    dot_general x1, matrix products, body(): jnp.einsum('fhqk,fkhd->fhqd', weights, value_heads, preferred_element_typ...  9.53 us
    ppermute x1, waiting for transfers between devices, padded_2(): lax.ppermute(lax.slice_in_dim(block, block.shape[dim] - width, None, axis...  8.76 us
    reduce_sum x2, other arithmetic, layer_norm(): spread = jnp.mean(shifted * shifted, axis=-1, keepdims=True)  7.93 us
  transfers between devices with their start and end apart: 4, of which 3 were waited for; matrix products, arithmetic and copies ran while one was open for 5% of the time, Pallas kernels for 0%

commit v1 on v0

--- a/solution.py
+++ b/solution.py
@@ -89,8 +89,16 @@
     second = jnp.sum(grouped * grouped, axis=(0, 1, 2, 4))
     first, second = lax.psum((first, second), ("frame", "row"))
     number = frames * lax.axis_size("frame") * pixels * lax.axis_size("row") * per_group
-    hidden = normalize_silu(grouped, first, second, number, norm_gain, latent.shape)
-    padded = padded_2(hidden, (("frame", 0),), 1)
+    wide = padded_2(latent, (("frame", 0),), 1)
+    wide_frames = wide.shape[0]
+    wide_grouped = wide.astype(jnp.float32).reshape(
+        wide_frames, row_count, col_count, GROUPS, per_group
+    )
+    padded = normalize_silu(wide_grouped, first, second, number, norm_gain, wide.shape)
+    me, count = lax.axis_index("frame"), lax.axis_size("frame")
+    place = me * frames - 1 + jnp.arange(wide_frames)
+    inside = (place >= 0) & (place < count * frames)
+    padded = jnp.where(inside[:, None, None, None], padded, jnp.zeros((), padded.dtype))
     mixed = jnp.zeros((frames * pixels, channels), jnp.float32)
     for tap in range(3):
         window = padded[tap : tap + frames].reshape(-1, channels)
@@ -123,12 +131,12 @@
     attended = (partial_sum / weight_sum[..., None]).astype(jnp.bfloat16)
     attended = jnp.transpose(attended, (0, 2, 1, 3)).reshape(frames, pixels, channels)
     spaced = add_projected(stepped, attended, space_out)
-    moved = lax.all_to_all(spaced, "frame", split_axis=1, concat_axis=0, tiled=True)
-    normed = layer_norm(moved, time_norm)
-    queries, key_rows, values = project_three(normed, time_qkv)
+    normed = layer_norm(spaced, time_norm)
+    moved = lax.all_to_all(normed, "frame", split_axis=1, concat_axis=0, tiled=True)
+    queries, key_rows, values = project_three(moved, time_qkv)
     result = time_attend(queries, key_rows, values)
-    finished = add_projected(moved, result, time_out)
-    output = lax.all_to_all(finished, "frame", split_axis=0, concat_axis=1, tiled=True)
+    result = lax.all_to_all(result, "frame", split_axis=0, concat_axis=1, tiled=True)
+    output = add_projected(spaced, result, time_out)
     return output.reshape(frames, row_count, col_count, channels)
 
 

time: 233 us -> 193 us (0.83)
  waiting for transfers between devices: 26.2 us -> 6.39 us
  blocking collectives: 107 us -> 93.8 us
  local copies, waits for them, and re-layouts: 32.5 us -> 25.7 us
  other arithmetic: 18.6 us -> 16.2 us
    all_to_all x2, blocking collectives: 72.2 us -> 44.3 us  [the longest x1 23.7 us: body(): lax.all_to_all(normed, 'frame', split_axis=1, concat_axis=0, tiled=True)]
    psum x1, blocking collectives: 34.9 us -> 49.5 us  [body(): first, second = lax.psum((first, second), ('frame', 'row'))]
    ppermute x1, waiting for transfers between devices: 8.76 us -> 0.01 us  [padded_2(): lax.ppermute(lax.slice_in_dim(block, block.shape[dim] - width, None, axis...]
    reduce_sum x2, other arithmetic: 7.93 us -> 0.57 us  [layer_norm(): spread = jnp.mean(shifted * shifted, axis=-1, keepdims=True)]
    ppermute x1, waiting for transfers between devices: 6.69 us -> 0.01 us  [padded_2(): lax.ppermute(lax.slice_in_dim(block, 0, width, axis=dim), axis, backward)]
    unnamed x0 -> x1, other arithmetic: none -> 5.57 us
    all_gather x1, waiting for transfers between devices: 10.5 us -> 6.1 us  [body(): key_piece = lax.all_gather(key_rows, 'row', axis=1, tiled=True)]
    dot_general x2, matrix products: 1.58 us -> 4.18 us  [add_projected(): jnp.dot(attended.reshape(-1, channels), weight, preferred_element_type=jn...]
  transfers between devices with their start and end apart: 4 -> 4, of which waited for: 3 -> 1; matrix products, arithmetic and copies ran while one was open for 5% -> 6% of each run, Pallas kernels for 0% -> 0%
where the time goes in v1:
time: 193 us; the launch traced here: 192 us
  blocking collectives  93.8 us (49%)
  matrix products  29.7 us (15%)
  local copies, waits for them, and re-layouts  25.7 us (13%)
  other arithmetic  16.2 us (8%)
  between operations  13.8 us (7%)
  starting transfers between devices  6.55 us (3%)
  waiting for transfers between devices  6.39 us (3%)
    psum x1, blocking collectives, body(): first, second = lax.psum((first, second), ('frame', 'row'))  49.5 us
    all_to_all x1, blocking collectives, body(): lax.all_to_all(normed, 'frame', split_axis=1, concat_axis=0, tiled=True)  23.7 us
    all_to_all x1, blocking collectives, body(): lax.all_to_all(result, 'frame', split_axis=0, concat_axis=1, tiled=True)  20.6 us
    unnamed x32, local copies, waits for them, and re-layouts  9.47 us
    dot_general x1, matrix products, body(): jnp.einsum('fhqk,fkhd->fhqd', weights, value_heads, preferred_element_typ...  9.35 us
    all_gather x1, waiting for transfers between devices, body(): key_piece = lax.all_gather(key_rows, 'row', axis=1, tiled=True)  6.1 us
    unnamed x1, other arithmetic  5.57 us
    dot_general x2, matrix products, project_three(): jnp.dot(inputs.reshape(-1, channels), weight, preferred_element_type=jnp....  5.31 us
  transfers between devices with their start and end apart: 4, of which 1 were waited for; matrix products, arithmetic and copies ran while one was open for 6% of the time, Pallas kernels for 0%

profile of v1, /device:TPU:0, one launch (start us, length us, event | category | flops | bytes accessed | tf_op | source)
XLA Modules:
  0.0 192.2 jit_solution(7589339824454949340)
XLA Ops:
  6.5 5.0 %collective-permute-start = (bf16[1,8,64,640]{3,2,1,0:T(8,128)(2,1)}, bf16[1,8,64,640]{3,2,1,0:T(8,128)(2,1)S(1)}, u32[]{:S(2)}, u32[]{:S(2)}) collective-permute-start(bf16[1,8,64,640]{3,2,1,0:T(8,128)(2,1)} %param.9), channel_id=1, source_target_pairs={{0,2},{2,4},{4,6},{6,8},{8,10},{10,12},{12,14},{1,3},{3,5},{5,7},{... | collective-permute-start | bytes 1966088 | tf_op jit(solution)/shard_map/ppermute | solution.py:18
  14.6 49.5 %all-reduce = (f32[32]{0:T(128)S(1)}, f32[32]{0:T(128)S(1)}) all-reduce(f32[32]{0:T(128)S(1)} %reduce_sum.91, f32[32]{0:T(128)S(1)} %reduce_sum.88), channel_id=1, replica_groups=mesh['groups'=2,'frame'=8,'row'=2] {'frame','row'}, use_global_device_ids=true, to_apply=%region_5.6 | all-reduce | flops 64 | bytes 512 | tf_op jit(solution)/shard_map/psum | solution.py:90
  64.5 2.5 %fusion.8 = bf16[3,8,64,640]{3,2,1,0:T(8,128)(2,1)S(1)} fusion(bf16[1,8,64,640]{3,2,1,0:T(8,128)(2,1)} %collective-permute-done.1, bf16[1,8,64,640]{3,2,1,0:T(8,128)(2,1)} %param.9, bf16[1,8,64,640]{3,2,1,0:T(8,128)(2,1)S(1)} %collective-permute-done, f32[640]{0:T(1024)} %param.10, f32[640]{0:T(1024)S(1)} %mul.99, f32[640]{0:T(1024)S(1)} %sub.69, ...), kind=kLoop, calls=%fused_computation.15 | loop fusion | flops 11796480 | bytes 3939843 | tf_op jit(solution)/shard_map/jit(_where)/select_n | solution.py:101
  71.9 1.9 fusion.4
  75.8 6.1 %all-gather.3.cloned.1.call-done = bf16[1,1024,640]{2,1,0:T(8,128)(2,1)} async-done(((bf16[1,512,640]{2,1,0:T(8,128)(2,1)}), bf16[1,1024,640]{2,1,0:T(8,128)(2,1)}) %all-gather.3.cloned.1.call-update) | async-done | bytes 1310736 | tf_op jit(solution)/shard_map/all_gather | solution.py:114
  81.9 1.6 copy.51
  83.5 3.0 %multiply_reduce_fusion = (f32[10,512]{1,0:T(8,128)S(1)}, f32[10,512,1024]{2,1,0:T(8,128)S(1)}) fusion(bf16[512,10,64]{0,2,1:T(8,128)(2,1)S(1)} %bitcast.69, bf16[1024,10,64]{0,2,1:T(8,128)(2,1)S(1)} %bitcast.63), kind=kOutput, calls=%fused_computation.1 | convolution fusion | flops 681569280 | bytes 22958080 | tf_op jit(solution)/shard_map/fqhd,fkhd->fhqk/dot_general | solution.py:119
  86.5 4.6 %fusion = f32[10,512]{1,0:T(8,128)S(1)} fusion(f32[10,512,1024]{2,1,0:T(8,128)S(1)} %get-tuple-element.25, f32[10,512]{1,0:T(8,128)S(1)} %get-tuple-element.24), kind=kLoop, calls=%fused_computation.2 | loop fusion | flops 15723520 | bytes 21012480 | tf_op jit(solution)/shard_map/reduce_sum | solution.py:125
  91.1 3.0 %copy-done.2 = f32[10,512,1024]{2,1,0:T(8,128)} copy-done((f32[10,512,1024]{2,1,0:T(8,128)}, f32[10,512,1024]{2,1,0:T(8,128)S(1)}, u32[]{:S(2)}) %copy-start.2) | copy-done | bytes 20971544
  94.1 1.6 copy.52
  95.8 9.4 %divide_convert_fusion = bf16[10,512,64]{1,2,0:T(8,128)(2,1)S(1)} fusion(bf16[1024,10,64]{0,2,1:T(8,128)(2,1)S(1)} %bitcast.75, f32[10,512,1024]{2,1,0:T(8,128)} %copy-done.2, f32[10,512]{1,0:T(8,128)S(1)} %get-tuple-element.24, f32[10,512]{1,0:T(8,128)S(1)} %get-tuple-element.19, f32[10,512]{1,0:T(8,128)S(1)} %get-tuple-element.18), kind=kOutput, calls=%fused_computation.26 | convolution fusion | flops 687800320 | bytes 22999040 | tf_op jit(solution)/shard_map/fhqk,fkhd->fhqd/dot_general | solution.py:127
  106.6 2.1 %copy.73 = bf16[1,512,640]{2,0,1:T(2,128)(2,1)} copy(bf16[1,512,640]{2,1,0:T(8,128)(2,1)S(1)} %fusion.27) | data formatting | bytes 1310720 | tf_op jit(solution)/shard_map/convert_element_type | solution.py:38
  109.3 5.6 %reduce.17 = bf16[512,640]{1,0:T(8,128)(2,1)S(1)} reduce(bf16[512,1,640]{2,1,0:T(2,128)(2,1)} %bitcast.64, bf16[]{:T(256)} %broadcast.133), dimensions={1}, to_apply=%bitcast.61.reduce_sub_computation | reduce | bytes 1310722
  115.0 23.7 %all_to_all.8 = bf16[8,2,20480]{2,1,0:T(2,128)(2,1)S(1)} all-to-all(bf16[8,2,20480]{2,1,0:T(2,128)(2,1)S(1)} %reshape.213), channel_id=1, replica_groups=mesh['groups'=2,'frame'=8,'row'=2] {'frame'}, dimensions={0} | all-to-all | bytes 1310720 | tf_op jit(solution)/shard_map/all_to_all | solution.py:135
  139.4 3.4 %convolution_convert_fusion = bf16[512,1920]{1,0:T(8,128)(2,1)S(1)} fusion(bf16[640,1920]{1,0:T(8,128)(2,1)} %param.16, bf16[1,512,640]{2,0,1:T(2,128)(2,1)S(1)} %bitcast.76), kind=kOutput, calls=%fused_computation.6 | convolution fusion | flops 1259274240 | bytes 5079040 | tf_op jit(solution)/shard_map/dot_general | solution.py:44
  143.9 1.6 copy.66
  145.6 1.7 copy.57
  148.0 1.6 copy.58
  150.4 1.7 copy.59
  152.1 2.8 %multiply_reduce_fusion.1 = (f32[64,10,8]{2,1,0:T(8,128)S(1)}, f32[64,10,8,8]{2,3,1,0:T(8,128)S(1)}) fusion(bf16[8,64,10,64]{3,0,2,1:T(8,128)(2,1)} %copy.57, bf16[8,64,10,64]{3,0,2,1:T(8,128)(2,1)} %copy.58), kind=kOutput, calls=%fused_computation.12 | convolution fusion | flops 5319680 | bytes 1495040 | tf_op jit(solution)/shard_map/qphd,kphd->phqk/dot_general | solution.py:61
  156.3 2.5 %fusion.5 = bf16[8,64,10,64]{3,0,2,1:T(8,128)(2,1)} fusion(bf16[8,64,10,64]{3,0,2,1:T(8,128)(2,1)S(1)} %copy-done.8, f32[64,10,8,8]{2,3,1,0:T(8,128)S(1)} %get-tuple-element.29, f32[8,64,10]{0,2,1:T(8,128)S(1)} %bitcast.78, f32[64,10,8]{2,1,0:T(8,128)S(1)} %get-tuple-element.28), kind=kOutput, calls=%fused_computation.10 | convolution fusion | flops 6021120 | bytes 1515520 | tf_op jit(solution)/shard_map/phqk,kphd->qphd/dot_general | solution.py:67
  158.8 2.0 %copy.61 = bf16[8,64,10,64]{1,3,2,0:T(8,128)(2,1)S(1)} copy(bf16[8,64,10,64]{3,0,2,1:T(8,128)(2,1)} %fusion.5) | data formatting | bytes 1310720 | tf_op jit(solution)/shard_map/convert_element_type | solution.py:69
  161.4 20.6 %all_to_all.9 = bf16[8,64,640]{2,1,0:T(8,128)(2,1)S(1)} all-to-all(bf16[8,64,640]{2,1,0:T(8,128)(2,1)S(1)} %copy.62), channel_id=1, replica_groups=mesh['groups'=2,'frame'=8,'row'=2] {'frame'}, dimensions={0} | all-to-all | bytes 1310720 | tf_op jit(solution)/shard_map/all_to_all | solution.py:138
  182.0 3.3 %convolution_add_fusion = f32[512,640]{1,0:T(8,128)} fusion(f32[512,640]{1,0:T(8,128)} %copy-done.3, bf16[512,640]{1,0:T(8,128)(2,1)S(1)} %bitcast.70, bf16[640,640]{1,0:T(8,128)(2,1)S(1)} %copy-done.10), kind=kOutput, calls=%fused_computation.16 | convolution fusion | flops 419758080 | bytes 4096000 | tf_op jit(solution)/shard_map/dot_general | solution.py:74
  (67 shorter events, 17.5 us)
Async XLA Ops:
  6.5 65.3 %copy-start = (bf16[640,1920]{1,0:T(8,128)(2,1)S(1)}, bf16[640,1920]{1,0:T(8,128)(2,1)}, u32[]{:S(2)}) copy-start(bf16[640,1920]{1,0:T(8,128)(2,1)} %param.13) | copy-start | bytes 7372804
  6.5 75.3 %all-gather.3.cloned.1.call-start = ((), (), s32[]{:S(2)}) async-start(), calls=%async_computation.2 | async-start | bytes 1966080 | tf_op jit(solution)/shard_map/all_gather | solution.py:114
  6.5 58.0 %collective-permute-start = (bf16[1,8,64,640]{3,2,1,0:T(8,128)(2,1)}, bf16[1,8,64,640]{3,2,1,0:T(8,128)(2,1)S(1)}, u32[]{:S(2)}, u32[]{:S(2)}) collective-permute-start(bf16[1,8,64,640]{3,2,1,0:T(8,128)(2,1)} %param.9), channel_id=1, source_target_pairs={{0,2},{2,4},{4,6},{6,8},{8,10},{10,12},{12,14},{1,3},{3,5},{5,7},{... | collective-permute-start | bytes 1966088 | tf_op jit(solution)/shard_map/ppermute | solution.py:18
  11.6 52.9 %collective-permute-start.1 = (bf16[1,8,64,640]{3,2,1,0:T(8,128)(2,1)}, bf16[1,8,64,640]{3,2,1,0:T(8,128)(2,1)}, u32[]{:S(2)}, u32[]{:S(2)}) collective-permute-start(bf16[1,8,64,640]{3,2,1,0:T(8,128)(2,1)} %param.9), channel_id=1, source_target_pairs={{2,0},{4,2},{6,4},{8,6},{10,8},{12,10},{14,12},{3,1},{5,3},{7,5},{... | collective-permute-start | bytes 1966088 | tf_op jit(solution)/shard_map/ppermute | solution.py:21
  67.0 1.7 copy-start.7
  69.5 1.1 copy-start.6
  70.6 1.3 copy-start.12
  71.5 2.2 %copy-start.4 = (f32[512,640]{1,0:T(8,128)}, f32[512,640]{1,0:T(8,128)S(1)}, u32[]{:S(2)}) copy-start(f32[512,640]{1,0:T(8,128)S(1)} %get-tuple-element.23) | copy-start | bytes 3932164
  75.0 19.1 %all-gather.5.cloned.1.call-start = ((), (), s32[]{:S(2)}) async-start(), calls=%async_computation.3 | async-start | bytes 1966080 | tf_op jit(solution)/shard_map/all_gather | solution.py:115
  86.5 7.6 %copy-start.2 = (f32[10,512,1024]{2,1,0:T(8,128)}, f32[10,512,1024]{2,1,0:T(8,128)S(1)}, u32[]{:S(2)}) copy-start(f32[10,512,1024]{2,1,0:T(8,128)S(1)} %get-tuple-element.25) | copy-start | bytes 62914564
  95.7 9.4 %copy-start.5 = (f32[512,640]{1,0:T(8,128)S(1)}, f32[512,640]{1,0:T(8,128)}, u32[]{:S(2)}) copy-start(f32[512,640]{1,0:T(8,128)} %copy-done.4) | copy-start | bytes 3932164
  95.8 9.4 %copy-start.9 = (bf16[640,640]{1,0:T(8,128)(2,1)S(1)}, bf16[640,640]{1,0:T(8,128)(2,1)}, u32[]{:S(2)}) copy-start(bf16[640,640]{1,0:T(8,128)(2,1)} %param.14) | copy-start | bytes 2457604
  105.2 1.2 copy-start.11
  106.1 2.6 %copy-start.3 = (f32[512,640]{1,0:T(8,128)}, f32[512,640]{1,0:T(8,128)S(1)}, u32[]{:S(2)}) copy-start(f32[512,640]{1,0:T(8,128)S(1)} %get-tuple-element.27) | copy-start | bytes 3932164
  154.9 1.3 copy-start.8
  160.8 21.2 %copy-start.10 = (bf16[640,640]{1,0:T(8,128)(2,1)S(1)}, bf16[640,640]{1,0:T(8,128)(2,1)}, u32[]{:S(2)}) copy-start(bf16[640,640]{1,0:T(8,128)(2,1)} %param.17) | copy-start | bytes 2457604
  182.0 3.3 %copy-start.1 = (bf16[640,1920]{1,0:T(8,128)(2,1)S(1)}, bf16[640,1920]{1,0:T(8,128)(2,1)}, u32[]{:S(2)}) copy-start(bf16[640,1920]{1,0:T(8,128)(2,1)} %param.13) | copy-start | bytes 7372804
Sparse Core Ops, SparseCore 0:
  75.1 6.6 all-gather.2
  83.4 10.5 all-gather.4

commit v2 on v0

v2 whole, which is shorter than its diff:
```python
import functools

import jax
import jax.numpy as jnp
from jax import lax
from jax.experimental import pallas as pl
from jax.experimental.pallas import tpu as pltpu
from jax.sharding import PartitionSpec as P

HEADS = 10
GROUPS = 32
MESH = pl.DeviceIdType.MESH
F32 = jnp.float32
BF16 = jnp.bfloat16

epsilon = 1e-05


def layer_norm(inputs, gain):
    center = jnp.mean(inputs, axis=-1, keepdims=True)
    shifted = inputs - center
    spread = jnp.mean(shifted * shifted, axis=-1, keepdims=True)
    return (shifted * lax.rsqrt(spread + epsilon) * gain).astype(BF16)


def dot(a, b):
    return jnp.dot(a, b, preferred_element_type=F32)


def dot_nt(a, b):
    return lax.dot_general(a, b, (((1,), (1,)), ((), ())), preferred_element_type=F32)


def kernel(
    frames, rows, chunks, number,
    latent, norm_gain, group_ones, time_kernel, space_norm, space_qkv, space_out, time_norm, time_qkv, time_out,
    out,
    own, near, far, stepped, tok_own, tok_other, q_all, k_all, v_all, nbuf, rbuf, abuf, obuf, part, stats,
    w_conv, w_sqkv, w_sout, w_tqkv, w_tout, att, q2, k2, v2, hid_scale,
    w_sem, stat_send, stat_recv, near_send, near_recv, far_send, far_recv, tok_send, tok_recv,
    fwd_send, fwd_recv, back_send, back_recv,
):
    me = lax.axis_index("frame")
    row = lax.axis_index("row")
    pixels, channels = own.shape
    size = pixels // chunks
    per = size // frames
    head = channels // HEADS
    pairs = HEADS // 2
    devices = frames * rows
    mine = me * rows + row
    odd = lax.rem(me, 2)
    partner = me + 1 - 2 * odd
    relay_to = me + 2 - 4 * odd
    far_from = me - 2 + 4 * odd
    relays = jnp.logical_and(relay_to >= 0, relay_to < frames)
    has_far = jnp.logical_and(far_from >= 0, far_from < frames)

    copies = [
        pltpu.make_async_copy(latent, own, w_sem.at[0]),
        pltpu.make_async_copy(time_kernel.at[1], w_conv.at[0], w_sem.at[1]),
        pltpu.make_async_copy(time_kernel.at[2 - 2 * odd], w_conv.at[1], w_sem.at[2]),
        pltpu.make_async_copy(time_kernel.at[2 * odd], w_conv.at[2], w_sem.at[3]),
        pltpu.make_async_copy(space_qkv, w_sqkv, w_sem.at[4]),
        pltpu.make_async_copy(space_out, w_sout, w_sem.at[5]),
        pltpu.make_async_copy(time_qkv, w_tqkv, w_sem.at[6]),
        pltpu.make_async_copy(time_out, w_tout, w_sem.at[7]),
    ]
    for copy in copies:
        copy.start()

    barrier = pltpu.get_barrier_semaphore()

    @pl.loop(1, devices)
    def _(i):
        peer = lax.rem(mine + i, devices)
        pl.semaphore_signal(
            barrier, inc=1, device_id={"frame": peer // rows, "row": lax.rem(peer, rows)}, device_id_type=MESH
        )

    copies[0].wait()
    first = jnp.zeros((1, channels), F32)
    second = jnp.zeros((1, channels), F32)
    for c in range(chunks):
        block = own[c * size : (c + 1) * size, :].astype(F32)
        first = first + jnp.sum(block, axis=0, keepdims=True)
        second = second + jnp.sum(block * block, axis=0, keepdims=True)
    part[...] = jnp.concatenate([first, second, jnp.zeros((6, channels), F32)], axis=0)
    pl.semaphore_wait(barrier, devices - 1)

    def near_copy(j):
        at = pl.ds(j * size, size)
        return pltpu.make_async_remote_copy(
            latent.at[at], near.at[at], near_send.at[j], near_recv.at[j],
            device_id={"frame": partner}, device_id_type=MESH,
        )

    def far_copy(j):
        at = pl.ds(j * size, size)
        return pltpu.make_async_remote_copy(
            near.at[at], far.at[at], far_send.at[j], far_recv.at[j],
            device_id={"frame": lax.max(0, lax.min(relay_to, frames - 1))}, device_id_type=MESH,
        )

    def tok_copy(j):
        at = pl.ds(j * size, size)
        return pltpu.make_async_remote_copy(
            tok_own.at[at], tok_other.at[at], tok_send.at[j], tok_recv.at[j],
            device_id={"row": 1 - row}, device_id_type=MESH,
        )

    def stat_copy(peer, slot):
        return pltpu.make_async_remote_copy(
            part, stats.at[slot], stat_send.at[peer], stat_recv.at[slot],
            device_id={"frame": peer // rows, "row": lax.rem(peer, rows)}, device_id_type=MESH,
        )

    @pl.loop(1, devices)
    def _(i):
        peer = lax.rem(mine + i, devices)
        stat_copy(peer, mine).start()

    @pl.loop(0, chunks)
    def _(j):
        near_copy(j).start()

    stats[mine] = part[...]

    @pl.loop(1, devices)
    def _(i):
        source = lax.rem(mine + i, devices)
        stat_copy(source, source).wait_recv()

    total = jnp.sum(stats[...], axis=0)
    grouped = jnp.dot(total, group_ones[...], preferred_element_type=F32, precision=lax.Precision.HIGHEST)
    center = grouped[0:1] / number
    spread = grouped[1:2] / number - center * center
    hid_scale[0:1, :] = center
    hid_scale[1:2, :] = lax.rsqrt(spread + epsilon) * norm_gain[...]

    def hidden(ref, c):
        block = ref[pl.ds(c * size, size), :].astype(F32)
        v = (block - hid_scale[0:1, :]) * hid_scale[1:2, :]
        return (v / (1.0 + jnp.exp(-v))).astype(BF16)

    copies[1].wait()

    @pl.loop(0, chunks)
    def _(c):
        at = pl.ds(c * size, size)
        stepped[at, :] = own[at, :].astype(F32) + dot(hidden(own, c), w_conv[0])

    for copy in copies[2:6]:
        copy.wait()

    scale = head ** (-0.5)

    @pl.loop(0, chunks + 1)
    def _(t):
        @pl.when(t < chunks)
        def _():
            near_copy(t).wait_recv()

            @pl.when(relays)
            def _():
                far_copy(t).start()

            at = pl.ds(t * size, size)
            stepped[at, :] += dot(hidden(near, t), w_conv[1])

        @pl.when(t >= 1)
        def _():
            c = t - 1
            at = pl.ds(c * size, size)

            @pl.when(has_far)
            def _():
                far_copy(c).wait_recv()
                stepped[at, :] += dot(hidden(far, c), w_conv[2])

            tok_own[at, :] = layer_norm(stepped[at, :], space_norm[...])
            tok_copy(c).start()
            tokens = tok_own[at, :]
            q_all[at, :] = (dot(tokens, w_sqkv[:, :channels]) * scale).astype(BF16)
            k_all[at, :] = dot(tokens, w_sqkv[:, channels : 2 * channels]).astype(BF16)
            v_all[at, :] = dot(tokens, w_sqkv[:, 2 * channels :]).astype(BF16)

    @pl.loop(0, chunks)
    def _(c):
        tok_copy(c).wait_recv()
        tokens = tok_other[pl.ds(c * size, size), :]
        to = pl.ds(pixels + c * size, size)
        k_all[to, :] = dot(tokens, w_sqkv[:, channels : 2 * channels]).astype(BF16)
        v_all[to, :] = dot(tokens, w_sqkv[:, 2 * channels :]).astype(BF16)

    for copy in copies[6:]:
        copy.wait()

    lane = lax.broadcasted_iota(jnp.int32, (1, 2 * head), 1)
    low = lane < head
    masks = (low.astype(F32).astype(BF16), (1.0 - low.astype(F32)).astype(BF16))

    def attend_pair(query, keys, values, same):
        results = []
        for mask in masks:
            scores = dot_nt(query * mask, keys)
            if same is not None:
                scores = jnp.where(same, scores, -jnp.inf)
            raised = jnp.exp(scores - jnp.max(scores, axis=-1, keepdims=True))
            weight_sum = jnp.sum(raised, axis=-1, keepdims=True)
            results.append(dot(raised.astype(BF16), values) / weight_sum)
        return jnp.where(low, results[0], results[1]).astype(BF16)

    def slot(c, f):
        return pl.ds(pl.multiple_of(c * size + f * per, per), per)

    def fwd_copy(c, dest, source):
        return pltpu.make_async_remote_copy(
            nbuf.at[slot(c, dest)], rbuf.at[slot(c, source)],
            fwd_send.at[c, dest], fwd_recv.at[c, source],
            device_id={"frame": dest}, device_id_type=MESH,
        )

    def back_copy(c, dest, source):
        return pltpu.make_async_remote_copy(
            abuf.at[slot(c, dest)], obuf.at[slot(c, source)],
            back_send.at[c, dest], back_recv.at[c, source],
            device_id={"frame": dest}, device_id_type=MESH,
        )

    @pl.loop(0, chunks + 2)
    def _(t):
        @pl.when(t < chunks)
        def _():
            c = t
            at = pl.ds(c * size, size)
            for p in range(pairs):
                block = slice(p * 2 * head, (p + 1) * 2 * head)
                att[:, block] = attend_pair(q_all[at, block], k_all[:, block], v_all[:, block], None)
            spaced = stepped[at, :] + dot(att[...], w_sout[...])
            stepped[at, :] = spaced
            nbuf[at, :] = layer_norm(spaced, time_norm[...])

            @pl.loop(1, frames)
            def _(i):
                fwd_copy(c, lax.rem(me + i, frames), me).start()

            rbuf[slot(c, me), :] = nbuf[slot(c, me), :]

        @pl.when(jnp.logical_and(t >= 1, t <= chunks))
        def _():
            c = t - 1
            at = pl.ds(c * size, size)

            @pl.loop(1, frames)
            def _(i):
                source = lax.rem(me + i, frames)
                fwd_copy(c, source, source).wait_recv()

            tokens = rbuf[at, :]
            q2[...] = (dot(tokens, w_tqkv[:, :channels]) * scale).astype(BF16)
            k2[...] = dot(tokens, w_tqkv[:, channels : 2 * channels]).astype(BF16)
            v2[...] = dot(tokens, w_tqkv[:, 2 * channels :]).astype(BF16)
            across = lax.broadcasted_iota(jnp.int32, (size, size), 1)
            down = lax.broadcasted_iota(jnp.int32, (size, size), 0)
            same = lax.rem(across, per) == lax.rem(down, per)
            for p in range(pairs):
                block = slice(p * 2 * head, (p + 1) * 2 * head)
                abuf[at, block] = attend_pair(q2[:, block], k2[:, block], v2[:, block], same)

            @pl.loop(1, frames)
            def _(i):
                back_copy(c, lax.rem(me + i, frames), me).start()

            obuf[slot(c, me), :] = abuf[slot(c, me), :]

        @pl.when(t >= 2)
        def _():
            c = t - 2
            at = pl.ds(c * size, size)

            @pl.loop(1, frames)
            def _(i):
                source = lax.rem(me + i, frames)
                back_copy(c, source, source).wait_recv()

            out[at, :] = stepped[at, :] + dot(obuf[at, :], w_tout[...])

    @pl.loop(1, devices)
    def _(i):
        peer = lax.rem(mine + i, devices)
        stat_copy(peer, mine).wait_send()

    @pl.loop(0, chunks)
    def _(c):
        near_copy(c).wait_send()
        tok_copy(c).wait_send()

        @pl.when(relays)
        def _():
            far_copy(c).wait_send()

        @pl.loop(1, frames)
        def _(i):
            dest = lax.rem(me + i, frames)
            fwd_copy(c, dest, me).wait_send()
            back_copy(c, dest, me).wait_send()


def body(
    frames, rows,
    latent, norm_gain, time_kernel, space_norm, space_qkv, space_out, time_norm, time_qkv, time_out,
):
    held, row_count, col_count, channels = latent.shape
    pixels = held * row_count * col_count
    per_group = channels // GROUPS
    chunks = max(1, pixels // (16 * frames))
    size = pixels // chunks
    number = float(frames * rows * pixels * per_group)
    group = jnp.arange(channels) // per_group
    group_ones = (group[:, None] == group[None, :]).astype(F32)
    devices = frames * rows
    vmem = pl.BlockSpec(memory_space=pltpu.VMEM)
    hbm = pl.BlockSpec(memory_space=pl.ANY)

    def wide(n=pixels, kind=BF16, width=channels):
        return pltpu.VMEM((n, width), kind)

    dma = pltpu.SemaphoreType.DMA
    output = pl.pallas_call(
        functools.partial(kernel, frames, rows, chunks, number),
        out_shape=jax.ShapeDtypeStruct((pixels, channels), F32),
        in_specs=[hbm, vmem, vmem, hbm, vmem, hbm, hbm, vmem, hbm, hbm],
        out_specs=vmem,
        scratch_shapes=[
            wide(), wide(), wide(), wide(kind=F32), wide(), wide(), wide(), wide(2 * pixels), wide(2 * pixels),
            wide(), wide(), wide(), wide(),
            pltpu.VMEM((8, channels), F32),
            pltpu.VMEM((devices, 8, channels), F32),
            pltpu.VMEM((3, channels, channels), BF16),
            wide(channels, BF16, 3 * channels), wide(channels),
            wide(channels, BF16, 3 * channels), wide(channels),
            wide(size), wide(size), wide(size), wide(size),
            pltpu.VMEM((8, channels), F32),
            dma((8,)), dma((devices,)), dma((devices,)),
            dma((chunks,)), dma((chunks,)), dma((chunks,)), dma((chunks,)), dma((chunks,)), dma((chunks,)),
            dma((chunks, frames)), dma((chunks, frames)), dma((chunks, frames)), dma((chunks, frames)),
        ],
        compiler_params=pltpu.CompilerParams(
            collective_id=0, has_side_effects=True, vmem_limit_bytes=60 * 1024 * 1024
        ),
    )(
        latent.reshape(pixels, channels), norm_gain[None], group_ones, time_kernel, space_norm[None], space_qkv,
        space_out, time_norm[None], time_qkv, time_out,
    )
    return output.reshape(latent.shape)


def solution(mesh):
    frames, rows = mesh.shape["frame"], mesh.shape["row"]
    split = P(("groups", "frame"), "row", None, None)
    return jax.shard_map(
        functools.partial(body, frames, rows),
        mesh=mesh,
        in_specs=(split, P(), P(), P(), P(), P(), P(), P(), P()),
        out_specs=split,
        check_vma=False,
    )
```

time: 233 us -> 85.4 us (0.37)
  blocking collectives: 107 us -> 0 us
  Pallas kernels: 0 us -> 77.5 us
  matrix products: 28.6 us -> 0 us
  local copies, waits for them, and re-layouts: 32.5 us -> 6.26 us
  waiting for transfers between devices: 26.2 us -> 0 us
  other arithmetic: 18.6 us -> 1.38 us
  between operations: 13.7 us -> 0.01 us
  starting transfers between devices: 6.1 us -> 0 us
    pallas_call x0 -> x1, Pallas kernels: none -> 77.5 us  [body(): pl.pallas_call(functools.partial(kernel, frames, rows, chunks, number), o...]
    all_to_all x2 -> x0, blocking collectives: 72.2 us -> none  [the longest x1 37.4 us: body(): lax.all_to_all(spaced, 'frame', split_axis=1, concat_axis=0, tiled=True)]
    psum x1 -> x0, blocking collectives: 34.9 us -> none  [body(): first, second = lax.psum((first, second), ('frame', 'row'))]
    dot_general x11 -> x0, matrix products: 28.6 us -> none  [the longest x1 9.53 us: body(): jnp.einsum('fhqk,fkhd->fhqd', weights, value_heads, preferred_element_typ...]
    reduce_sum x8 -> x0, other arithmetic: 17 us -> none  [the longest x2 7.93 us: layer_norm(): spread = jnp.mean(shifted * shifted, axis=-1, keepdims=True)]
    ppermute x2 -> x0, waiting for transfers between devices: 15.4 us -> none  [the longest x1 8.76 us: padded_2(): lax.ppermute(lax.slice_in_dim(block, block.shape[dim] - width, None, axis...]
    all_gather x2 -> x0, waiting for transfers between devices: 10.5 us -> none  [the longest x1 10.5 us: body(): key_piece = lax.all_gather(key_rows, 'row', axis=1, tiled=True)]
    reshape x4 -> x0, local copies, waits for them, and re-layouts: 9.24 us -> none  [the longest x1 2.65 us: time_attend(): value_heads = values.reshape(frames, pixels, HEADS, head_size)]
  transfers between devices with their start and end apart: 4 -> 0, of which waited for: 3 -> 0; matrix products, arithmetic and copies ran while one was open for 5% -> 0% of each run, Pallas kernels for 0% -> 0%
where the time goes in v2:
time: 85.4 us; the launch traced here: 85.1 us
  Pallas kernels  77.5 us (91%)
  local copies, waits for them, and re-layouts  6.26 us (7%)
  other arithmetic  1.38 us (2%)
    pallas_call x1, Pallas kernels, body(): pl.pallas_call(functools.partial(kernel, frames, rows, chunks, number), o...  77.5 us
    unnamed x1, local copies, waits for them, and re-layouts  2.47 us

profile of v2, /device:TPU:0, one launch (start us, length us, event | category | flops | bytes accessed | tf_op | source)
XLA Modules:
  0.0 85.1 jit_solution(8717446040983340875)
XLA Ops:
  0.0 1.3 %broadcast_in_dim.11.norm_gain = f32[1,640]{1,0:T(1,128)} reshape(f32[640]{0:T(1024)} %param.10) | data formatting | bytes 5120 | tf_op jit(solution)/shard_map/broadcast_in_dim | solution.py:353
  1.3 1.3 %broadcast_in_dim.12.space_norm = f32[1,640]{1,0:T(1,128)} reshape(f32[640]{0:T(1024)} %param.12) | data formatting | bytes 5120 | tf_op jit(solution)/shard_map/broadcast_in_dim | solution.py:353
  2.5 1.3 %broadcast_in_dim.13.time_norm = f32[1,640]{1,0:T(1,128)} reshape(f32[640]{0:T(1024)} %param.15) | data formatting | bytes 5120 | tf_op jit(solution)/shard_map/broadcast_in_dim | solution.py:354
  3.8 1.4 %compare_convert_fusion.group_ones = f32[640,640]{1,0:T(8,128)} fusion(s32[640]{0:T(1024)S(1)} %add_select_fusion), kind=kLoop, calls=%fused_computation | loop fusion | flops 819200 | bytes 1640960 | tf_op jit(solution)/shard_map/convert_element_type | solution.py:321
  5.2 77.5 %shard_map.91 = f32[512,640]{1,0:T(8,128)} custom-call(bf16[512,640]{1,0:T(8,128)(2,1)} %bitcast.3, f32[1,640]{1,0:T(1,128)} %broadcast_in_dim.11.norm_gain, f32[640,640]{1,0:T(8,128)} %compare_convert_fusion.group_ones, bf16[3,640,640]{2,1,0:T(8,128)(2,1)} %time_kernel.1, f32[1,640]{1,0:T(1,128)} %broadcast_in_dim.12.space_norm, ...), custom_call_target="tpu_custom_call" | custom-call | tf_op jit(solution)/shard_map/pallas_call | solution.py:330
  82.7 2.5 %copy.11 = f32[1,8,64,640]{3,2,1,0:T(8,128)} copy(f32[1,8,64,640]{3,2,1,0:T(8,128)} %bitcast.2) | data formatting | bytes 2621440
  (1 shorter events, 0.0 us)

commit v3 on v2

--- a/solution.py
+++ b/solution.py
@@ -32,13 +32,13 @@
 
 
 def kernel(
-    frames, rows, chunks, number,
-    latent, norm_gain, group_ones, time_kernel, space_norm, space_qkv, space_out, time_norm, time_qkv, time_out,
+    frames, rows, chunks, number, per_group,
+    latent, norm_gain, time_kernel, space_norm, space_qkv, space_out, time_norm, time_qkv, time_out,
     out,
     own, near, far, stepped, tok_own, tok_other, q_all, k_all, v_all, nbuf, rbuf, abuf, obuf, part, stats,
-    w_conv, w_sqkv, w_sout, w_tqkv, w_tout, att, q2, k2, v2, hid_scale,
+    w_conv, w_sqkv, w_sout, w_tqkv, w_tout, att, q2, k2, v2, hid_scale, group_ones,
     w_sem, stat_send, stat_recv, near_send, near_recv, far_send, far_recv, tok_send, tok_recv,
-    fwd_send, fwd_recv, back_send, back_recv,
+    fwd_send, fwd_recv, back_send, back_recv, out_sem,
 ):
     me = lax.axis_index("frame")
     row = lax.axis_index("row")
@@ -86,6 +86,11 @@
         first = first + jnp.sum(block, axis=0, keepdims=True)
         second = second + jnp.sum(block * block, axis=0, keepdims=True)
     part[...] = jnp.concatenate([first, second, jnp.zeros((6, channels), F32)], axis=0)
+    down = lax.broadcasted_iota(jnp.int32, (channels, channels), 0)
+    start = down - lax.rem(down, per_group)
+    across = lax.broadcasted_iota(jnp.int32, (channels, channels), 1)
+    inside = jnp.logical_and(across >= start, across < start + per_group)
+    group_ones[...] = jnp.where(inside, 1.0, 0.0).astype(BF16)
     pl.semaphore_wait(barrier, devices - 1)
 
     def near_copy(j):
@@ -132,11 +137,15 @@
         stat_copy(source, source).wait_recv()
 
     total = jnp.sum(stats[...], axis=0)
-    grouped = jnp.dot(total, group_ones[...], preferred_element_type=F32, precision=lax.Precision.HIGHEST)
+    high = total.astype(BF16).astype(F32)
+    middle = (total - high).astype(BF16).astype(F32)
+    lowest = total - high - middle
+    pieces = dot(jnp.concatenate([high, middle, lowest], axis=0).astype(BF16), group_ones[...])
+    grouped = pieces[0:8] + pieces[8:16] + pieces[16:24]
     center = grouped[0:1] / number
     spread = grouped[1:2] / number - center * center
     hid_scale[0:1, :] = center
-    hid_scale[1:2, :] = lax.rsqrt(spread + epsilon) * norm_gain[...]
+    hid_scale[1:2, :] = lax.rsqrt(spread + epsilon) * norm_gain[...].reshape(1, channels)
 
     def hidden(ref, c):
         block = ref[pl.ds(c * size, size), :].astype(F32)
@@ -155,7 +164,7 @@
 
     scale = head ** (-0.5)
 
-    @pl.loop(0, chunks + 1)
+    @pl.loop(0, chunks + 2)
     def _(t):
         @pl.when(t < chunks)
         def _():
@@ -168,7 +177,7 @@
             at = pl.ds(t * size, size)
             stepped[at, :] += dot(hidden(near, t), w_conv[1])
 
-        @pl.when(t >= 1)
+        @pl.when(jnp.logical_and(t >= 1, t <= chunks))
         def _():
             c = t - 1
             at = pl.ds(c * size, size)
@@ -178,20 +187,21 @@
                 far_copy(c).wait_recv()
                 stepped[at, :] += dot(hidden(far, c), w_conv[2])
 
-            tok_own[at, :] = layer_norm(stepped[at, :], space_norm[...])
+            tok_own[at, :] = layer_norm(stepped[at, :], space_norm[...].reshape(1, channels))
             tok_copy(c).start()
             tokens = tok_own[at, :]
             q_all[at, :] = (dot(tokens, w_sqkv[:, :channels]) * scale).astype(BF16)
             k_all[at, :] = dot(tokens, w_sqkv[:, channels : 2 * channels]).astype(BF16)
             v_all[at, :] = dot(tokens, w_sqkv[:, 2 * channels :]).astype(BF16)
 
-    @pl.loop(0, chunks)
-    def _(c):
-        tok_copy(c).wait_recv()
-        tokens = tok_other[pl.ds(c * size, size), :]
-        to = pl.ds(pixels + c * size, size)
-        k_all[to, :] = dot(tokens, w_sqkv[:, channels : 2 * channels]).astype(BF16)
-        v_all[to, :] = dot(tokens, w_sqkv[:, 2 * channels :]).astype(BF16)
+        @pl.when(t >= 2)
+        def _():
+            c = t - 2
+            tok_copy(c).wait_recv()
+            tokens = tok_other[pl.ds(c * size, size), :]
+            to = pl.ds(pixels + c * size, size)
+            k_all[to, :] = dot(tokens, w_sqkv[:, channels : 2 * channels]).astype(BF16)
+            v_all[to, :] = dot(tokens, w_sqkv[:, 2 * channels :]).astype(BF16)
 
     for copy in copies[6:]:
         copy.wait()
@@ -201,15 +211,14 @@
     masks = (low.astype(F32).astype(BF16), (1.0 - low.astype(F32)).astype(BF16))
 
     def attend_pair(query, keys, values, same):
-        results = []
-        for mask in masks:
-            scores = dot_nt(query * mask, keys)
-            if same is not None:
-                scores = jnp.where(same, scores, -jnp.inf)
-            raised = jnp.exp(scores - jnp.max(scores, axis=-1, keepdims=True))
-            weight_sum = jnp.sum(raised, axis=-1, keepdims=True)
-            results.append(dot(raised.astype(BF16), values) / weight_sum)
-        return jnp.where(low, results[0], results[1]).astype(BF16)
+        both = jnp.concatenate([query * mask for mask in masks], axis=0)
+        scores = dot_nt(both, keys)
+        if same is not None:
+            scores = jnp.where(same, scores, -jnp.inf)
+        raised = jnp.exp(scores - jnp.max(scores, axis=-1, keepdims=True))
+        weight_sum = jnp.sum(raised, axis=-1, keepdims=True)
+        result = dot(raised.astype(BF16), values) / weight_sum
+        return jnp.where(low, result[:size], result[size:]).astype(BF16)
 
     def slot(c, f):
         return pl.ds(pl.multiple_of(c * size + f * per, per), per)
@@ -220,6 +229,10 @@
             fwd_send.at[c, dest], fwd_recv.at[c, source],
             device_id={"frame": dest}, device_id_type=MESH,
         )
+
+    def out_copy(c):
+        at = pl.ds(c * size, size)
+        return pltpu.make_async_copy(stepped.at[at], out.at[at], out_sem.at[c])
 
     def back_copy(c, dest, source):
         return pltpu.make_async_remote_copy(
@@ -239,7 +252,7 @@
                 att[:, block] = attend_pair(q_all[at, block], k_all[:, block], v_all[:, block], None)
             spaced = stepped[at, :] + dot(att[...], w_sout[...])
             stepped[at, :] = spaced
-            nbuf[at, :] = layer_norm(spaced, time_norm[...])
+            nbuf[at, :] = layer_norm(spaced, time_norm[...].reshape(1, channels))
 
             @pl.loop(1, frames)
             def _(i):
@@ -261,8 +274,8 @@
             q2[...] = (dot(tokens, w_tqkv[:, :channels]) * scale).astype(BF16)
             k2[...] = dot(tokens, w_tqkv[:, channels : 2 * channels]).astype(BF16)
             v2[...] = dot(tokens, w_tqkv[:, 2 * channels :]).astype(BF16)
-            across = lax.broadcasted_iota(jnp.int32, (size, size), 1)
-            down = lax.broadcasted_iota(jnp.int32, (size, size), 0)
+            across = lax.broadcasted_iota(jnp.int32, (2 * size, size), 1)
+            down = lax.broadcasted_iota(jnp.int32, (2 * size, size), 0)
             same = lax.rem(across, per) == lax.rem(down, per)
             for p in range(pairs):
                 block = slice(p * 2 * head, (p + 1) * 2 * head)
@@ -284,7 +297,8 @@
                 source = lax.rem(me + i, frames)
                 back_copy(c, source, source).wait_recv()
 
-            out[at, :] = stepped[at, :] + dot(obuf[at, :], w_tout[...])
+            stepped[at, :] += dot(obuf[at, :], w_tout[...])
+            out_copy(c).start()
 
     @pl.loop(1, devices)
     def _(i):
@@ -294,6 +308,7 @@
     @pl.loop(0, chunks)
     def _(c):
         near_copy(c).wait_send()
+        out_copy(c).wait()
         tok_copy(c).wait_send()
 
         @pl.when(relays)
@@ -317,8 +332,6 @@
     chunks = max(1, pixels // (16 * frames))
     size = pixels // chunks
     number = float(frames * rows * pixels * per_group)
-    group = jnp.arange(channels) // per_group
-    group_ones = (group[:, None] == group[None, :]).astype(F32)
     devices = frames * rows
     vmem = pl.BlockSpec(memory_space=pltpu.VMEM)
     hbm = pl.BlockSpec(memory_space=pl.ANY)
@@ -328,10 +341,10 @@
 
     dma = pltpu.SemaphoreType.DMA
     output = pl.pallas_call(
-        functools.partial(kernel, frames, rows, chunks, number),
+        functools.partial(kernel, frames, rows, chunks, number, per_group),
         out_shape=jax.ShapeDtypeStruct((pixels, channels), F32),
-        in_specs=[hbm, vmem, vmem, hbm, vmem, hbm, hbm, vmem, hbm, hbm],
-        out_specs=vmem,
+        in_specs=[hbm, vmem, hbm, vmem, hbm, hbm, vmem, hbm, hbm],
+        out_specs=hbm,
         scratch_shapes=[
             wide(), wide(), wide(), wide(kind=F32), wide(), wide(), wide(), wide(2 * pixels), wide(2 * pixels),
             wide(), wide(), wide(), wide(),
@@ -342,16 +355,17 @@
             wide(channels, BF16, 3 * channels), wide(channels),
             wide(size), wide(size), wide(size), wide(size),
             pltpu.VMEM((8, channels), F32),
+            wide(channels),
             dma((8,)), dma((devices,)), dma((devices,)),
             dma((chunks,)), dma((chunks,)), dma((chunks,)), dma((chunks,)), dma((chunks,)), dma((chunks,)),
-            dma((chunks, frames)), dma((chunks, frames)), dma((chunks, frames)), dma((chunks, frames)),
+            dma((chunks, frames)), dma((chunks, frames)), dma((chunks, frames)), dma((chunks, frames)), dma((chunks,)),
         ],
         compiler_params=pltpu.CompilerParams(
             collective_id=0, has_side_effects=True, vmem_limit_bytes=60 * 1024 * 1024
         ),
     )(
-        latent.reshape(pixels, channels), norm_gain[None], group_ones, time_kernel, space_norm[None], space_qkv,
-        space_out, time_norm[None], time_qkv, time_out,
+        latent.reshape(pixels, channels), norm_gain, time_kernel, space_norm, space_qkv,
+        space_out, time_norm, time_qkv, time_out,
     )
     return output.reshape(latent.shape)
 

time: 85.4 us -> 74.7 us (0.87)
  Pallas kernels: 77.5 us -> 72.1 us
  local copies, waits for them, and re-layouts: 6.26 us -> 2.47 us
  other arithmetic: 1.38 us -> 0 us
    pallas_call x1, Pallas kernels: 77.5 us -> 72.1 us  [body(): pl.pallas_call(functools.partial(kernel, frames, rows, chunks, number, pe...]
    broadcast_in_dim x3 -> x0, local copies, waits for them, and re-layouts: 3.78 us -> none  [the longest x1 1.27 us: body(): norm_gain[None]]
    convert_element_type x1 -> x0, other arithmetic: 1.37 us -> none  [body(): group_ones = (group[:, None] == group[None, :]).astype(F32)]
where the time goes in v3:
time: 74.7 us; the launch traced here: 74.5 us
  Pallas kernels  72.1 us (97%)
  local copies, waits for them, and re-layouts  2.47 us (3%)
    pallas_call x1, Pallas kernels, body(): pl.pallas_call(functools.partial(kernel, frames, rows, chunks, number, pe...  72.1 us
    unnamed x1, local copies, waits for them, and re-layouts  2.47 us

profile of v3, /device:TPU:0, one launch (start us, length us, event | category | flops | bytes accessed | tf_op | source)
XLA Modules:
  0.0 74.5 jit_solution(11411204380064863389)
XLA Ops:
  0.0 72.1 %shard_map.91 = f32[512,640]{1,0:T(8,128)} custom-call(bf16[512,640]{1,0:T(8,128)(2,1)} %bitcast.3, f32[640]{0:T(1024)} %norm_gain.1, bf16[3,640,640]{2,1,0:T(8,128)(2,1)} %time_kernel.1, f32[640]{0:T(1024)} %space_norm.1, bf16[640,1920]{1,0:T(8,128)(2,1)} %space_qkv.1, bf16[640,640]{1,0:T(8,128)(2,1)} %space_out.1, f32[640]{0:T(1024)} %time_norm.1, ...), custom_call_target="tpu_custom_call" | custom-call | tf_op jit(solution)/shard_map/pallas_call | solution.py:343
  72.1 2.5 %copy.11 = f32[1,8,64,640]{3,2,1,0:T(8,128)} copy(f32[1,8,64,640]{3,2,1,0:T(8,128)} %bitcast.2) | data formatting | bytes 2621440

commit v4 on v3

--- a/solution.py
+++ b/solution.py
@@ -241,7 +241,7 @@
             device_id={"frame": dest}, device_id_type=MESH,
         )
 
-    @pl.loop(0, chunks + 2)
+    @pl.loop(0, chunks + 4)
     def _(t):
         @pl.when(t < chunks)
         def _():
@@ -260,9 +260,9 @@
 
             rbuf[slot(c, me), :] = nbuf[slot(c, me), :]
 
-        @pl.when(jnp.logical_and(t >= 1, t <= chunks))
-        def _():
-            c = t - 1
+        @pl.when(jnp.logical_and(t >= 2, t <= chunks + 1))
+        def _():
+            c = t - 2
             at = pl.ds(c * size, size)
 
             @pl.loop(1, frames)
@@ -287,9 +287,9 @@
 
             obuf[slot(c, me), :] = abuf[slot(c, me), :]
 
-        @pl.when(t >= 2)
-        def _():
-            c = t - 2
+        @pl.when(t >= 4)
+        def _():
+            c = t - 4
             at = pl.ds(c * size, size)
 
             @pl.loop(1, frames)

time: 74.7 us -> 73.1 us (0.979)
  Pallas kernels: 72.1 us -> 70.4 us
    pallas_call x1, Pallas kernels: 72.1 us -> 70.4 us  [body(): pl.pallas_call(functools.partial(kernel, frames, rows, chunks, number, pe...]
where the time goes in v4:
time: 73.1 us; the launch traced here: 72.9 us
  Pallas kernels  70.4 us (96%)
  local copies, waits for them, and re-layouts  2.47 us (3%)
    pallas_call x1, Pallas kernels, body(): pl.pallas_call(functools.partial(kernel, frames, rows, chunks, number, pe...  70.4 us
    unnamed x1, local copies, waits for them, and re-layouts  2.47 us

profile of v4, /device:TPU:0, one launch (start us, length us, event | category | flops | bytes accessed | tf_op | source)
XLA Modules:
  0.0 72.9 jit_solution(3104095404254371815)
XLA Ops:
  0.0 70.4 %shard_map.91 = f32[512,640]{1,0:T(8,128)} custom-call(bf16[512,640]{1,0:T(8,128)(2,1)} %bitcast.3, f32[640]{0:T(1024)} %norm_gain.1, bf16[3,640,640]{2,1,0:T(8,128)(2,1)} %time_kernel.1, f32[640]{0:T(1024)} %space_norm.1, bf16[640,1920]{1,0:T(8,128)(2,1)} %space_qkv.1, bf16[640,640]{1,0:T(8,128)(2,1)} %space_out.1, f32[640]{0:T(1024)} %time_norm.1, ...), custom_call_target="tpu_custom_call" | custom-call | tf_op jit(solution)/shard_map/pallas_call | solution.py:343
  70.4 2.5 %copy.11 = f32[1,8,64,640]{3,2,1,0:T(8,128)} copy(f32[1,8,64,640]{3,2,1,0:T(8,128)} %bitcast.2) | data formatting | bytes 2621440

commit v5 on v4

--- a/solution.py
+++ b/solution.py
@@ -147,17 +147,19 @@
     hid_scale[0:1, :] = center
     hid_scale[1:2, :] = lax.rsqrt(spread + epsilon) * norm_gain[...].reshape(1, channels)
 
-    def hidden(ref, c):
+    def hidden(ref, c, size=size):
         block = ref[pl.ds(c * size, size), :].astype(F32)
         v = (block - hid_scale[0:1, :]) * hid_scale[1:2, :]
         return (v / (1.0 + jnp.exp(-v))).astype(BF16)
 
     copies[1].wait()
 
-    @pl.loop(0, chunks)
+    half = pixels // 2
+
+    @pl.loop(0, 2)
     def _(c):
-        at = pl.ds(c * size, size)
-        stepped[at, :] = own[at, :].astype(F32) + dot(hidden(own, c), w_conv[0])
+        at = pl.ds(c * half, half)
+        stepped[at, :] = own[at, :].astype(F32) + dot(hidden(own, c, half), w_conv[0])
 
     for copy in copies[2:6]:
         copy.wait()
@@ -176,6 +178,15 @@
 
             at = pl.ds(t * size, size)
             stepped[at, :] += dot(hidden(near, t), w_conv[1])
+
+        @pl.when(t >= 2)
+        def _():
+            c = t - 2
+            tok_copy(c).wait_recv()
+            tokens = tok_other[pl.ds(c * size, size), :]
+            to = pl.ds(pixels + c * size, size)
+            k_all[to, :] = dot(tokens, w_sqkv[:, channels : 2 * channels]).astype(BF16)
+            v_all[to, :] = dot(tokens, w_sqkv[:, 2 * channels :]).astype(BF16)
 
         @pl.when(jnp.logical_and(t >= 1, t <= chunks))
         def _():
@@ -193,15 +204,6 @@
             q_all[at, :] = (dot(tokens, w_sqkv[:, :channels]) * scale).astype(BF16)
             k_all[at, :] = dot(tokens, w_sqkv[:, channels : 2 * channels]).astype(BF16)
             v_all[at, :] = dot(tokens, w_sqkv[:, 2 * channels :]).astype(BF16)
-
-        @pl.when(t >= 2)
-        def _():
-            c = t - 2
-            tok_copy(c).wait_recv()
-            tokens = tok_other[pl.ds(c * size, size), :]
-            to = pl.ds(pixels + c * size, size)
-            k_all[to, :] = dot(tokens, w_sqkv[:, channels : 2 * channels]).astype(BF16)
-            v_all[to, :] = dot(tokens, w_sqkv[:, 2 * channels :]).astype(BF16)
 
     for copy in copies[6:]:
         copy.wait()

time: 73.1 us -> 71.9 us (0.984)
  Pallas kernels: 70.4 us -> 69.3 us
    pallas_call x1, Pallas kernels: 70.4 us -> 69.3 us  [body(): pl.pallas_call(functools.partial(kernel, frames, rows, chunks, number, pe...]
where the time goes in v5:
time: 71.9 us; the launch traced here: 71.7 us
  Pallas kernels  69.3 us (96%)
  local copies, waits for them, and re-layouts  2.47 us (3%)
    pallas_call x1, Pallas kernels, body(): pl.pallas_call(functools.partial(kernel, frames, rows, chunks, number, pe...  69.3 us
    unnamed x1, local copies, waits for them, and re-layouts  2.47 us

profile of v5, /device:TPU:0, one launch (start us, length us, event | category | flops | bytes accessed | tf_op | source)
XLA Modules:
  0.0 71.7 jit_solution(16142737276780936301)
XLA Ops:
  0.0 69.3 %shard_map.91 = f32[512,640]{1,0:T(8,128)} custom-call(bf16[512,640]{1,0:T(8,128)(2,1)} %bitcast.3, f32[640]{0:T(1024)} %norm_gain.1, bf16[3,640,640]{2,1,0:T(8,128)(2,1)} %time_kernel.1, f32[640]{0:T(1024)} %space_norm.1, bf16[640,1920]{1,0:T(8,128)(2,1)} %space_qkv.1, bf16[640,640]{1,0:T(8,128)(2,1)} %space_out.1, f32[640]{0:T(1024)} %time_norm.1, ...), custom_call_target="tpu_custom_call" | custom-call | tf_op jit(solution)/shard_map/pallas_call | solution.py:345
  69.3 2.5 %copy.11 = f32[1,8,64,640]{3,2,1,0:T(8,128)} copy(f32[1,8,64,640]{3,2,1,0:T(8,128)} %bitcast.2) | data formatting | bytes 2621440
